TPU v7x, 32 devices: a whole 2x2x4 slice. The times are simulated.
32 devices in a mesh: ctx: 8 (over y, x, core), head: 4 (over z).
Axes of the slice: x: 2, y: 2, z: 4, core: 2. Of those that a mesh axis runs over, the one named last changes fastest.
Arguments:
- token_ids: int32 [2048], P('ctx'), may hold values from 0 to 31999
- labels: int32 [2048], P('ctx'), may hold values from 0 to 31999
- answer_mask: int32 [2048], P('ctx'), may hold values 0 or 1
- pair_map: int32 [8], replicated, may hold values from 0 to 7, each once
- w_layer: float32 [2048, 21504], P('ctx', 'head')
- w_vocab: float32 [2048, 64000], P('ctx', 'head')
- gains: float32 [2048, 3], P('ctx'), may hold values from 0.5 to 1.5
- mom_layer: float32 [2048, 21504], P('ctx', 'head'), may hold values from -1.1444092e-05 to 1.1444092e-05
- mom_vocab: float32 [2048, 64000], P('ctx', 'head'), may hold values from -1.1444092e-05 to 1.1444092e-05
- mom_gains: float32 [2048, 3], P('ctx'), may hold values from -1.1444092e-05 to 1.1444092e-05
- avg_layer: float32 [2048, 21504], P('ctx', 'head')
- avg_vocab: float32 [2048, 64000], P('ctx', 'head')
- avg_gains: float32 [2048, 3], P('ctx'), may hold values from 0.5 to 1.5
Outputs:
- layer_new: float32 [2048, 21504], P('ctx', 'head')
- layer_moment: float32 [2048, 21504], P('ctx', 'head')
- layer_average: float32 [2048, 21504], P('ctx', 'head')
- layer_copy: bfloat16 [2048, 21504], P('ctx', 'head')
- vocab_new: float32 [2048, 64000], P('ctx', 'head')
- vocab_moment: float32 [2048, 64000], P('ctx', 'head')
- vocab_average: float32 [2048, 64000], P('ctx', 'head')
- vocab_copy: bfloat16 [2048, 64000], P('ctx', 'head')
- gains_new: float32 [2048, 3], P('ctx')
- gains_moment: float32 [2048, 3], P('ctx')
- gains_average: float32 [2048, 3], P('ctx')
- gains_copy: bfloat16 [2048, 3], P('ctx')
- loss: float32 [], replicated
- grad_norm: float32 [], replicated
Inputs may be any that keep to these rules, and one draw needn't show every extreme that they name: `pair_map`: each index of ctx appears once.
All inputs are finite; a program needn't handle non-finite values. No bound on the sum of `answer_mask` on one device may be relied on, other than what follows from the above.
Results may differ from a plain program's by a relative error of at most 0.015.
The roundings to bfloat16 on the way count: a program that leaves them out, or rounds other values in their place, can miss the bound.
Values may be sent and summed in bfloat16 or wider, within the bound.
No kernel may reach another device: no remote copies, remote signals or barrier semaphores. Data moves between devices by JAX's collectives and lax.ppermute only.
A program may use at most 832 MiB of HBM per device.

v0:
```python
import math
import jax
import jax.numpy as jnp
from jax import lax
from jax.sharding import PartitionSpec as P

D = 2048
HEADS = 32
KV = 4
HD = 64
FF = 5632
V = 32000
SEQS = 2
eps = 1e-05
z_weight = 0.0001
momentum_rate = 0.5
average_rate = 0.5
clip_level = 0.01


def merged(value, axis, join):
    pieces = jax.tree.map(lambda part: lax.all_gather(part, axis), value)
    head = jax.tree.map(lambda part: part[0], pieces)
    tail = jax.tree.map(lambda part: part[1:], pieces)
    subtotal, _ = lax.scan(lambda subtotal, share: (join(subtotal, share), None), head, tail)
    return subtotal


def widths():
    group = HEADS // KV
    return (group, group * HD, FF // KV, V // KV)


def layer_spread(length):
    group, qg, ffg, vg = widths()
    attn_in = qg + 2 * HD
    column = jnp.arange(attn_in + qg + 3 * ffg)
    return jnp.where(
        column < attn_in,
        D ** (-0.5),
        jnp.where(
            column < attn_in + qg,
            (length / (4.0 * HEADS * HD)) ** 0.5,
            jnp.where(column < attn_in + qg + 2 * ffg, D ** (-0.5), FF ** (-0.5)),
        ),
    ).astype(jnp.float32)


def vocab_spread():
    vg = V // KV
    column = jnp.arange(2 * vg)
    return jnp.where(column < vg, 2.0 * D ** (-0.5), 1.0).astype(jnp.float32)


def total_params():
    return D * (2 * HEADS * HD + 2 * KV * HD + 3 * FF + 2 * V + 3)


def yarn_tables(positions, head_dim):
    half = head_dim // 2
    index = jnp.arange(half, dtype=jnp.float32)
    inverse = 10000.0 ** (-2.0 * index / head_dim)
    ratio = 2048.0 * inverse / (2.0 * math.pi)
    ramp = jnp.clip((ratio - 1.0) / 31.0, 0.0, 1.0)
    freq = (1.0 - ramp) * inverse / 4.0 + ramp * inverse
    angle = positions[:, None] * freq[None, :]
    mscale = 0.1 * math.log(4.0) + 1.0
    return (jnp.cos(angle) * mscale, jnp.sin(angle) * mscale)


def rope(x, cosine, sine):
    half = x.shape[-1] // 2
    first = x[..., :half]
    second = x[..., half:]
    return jnp.concatenate(
        [first * cosine - second * sine, second * cosine + first * sine], axis=-1
    )


def norm(x, gain):
    return x * lax.rsqrt(jnp.mean(x * x, axis=-1, keepdims=True) + eps) * gain


def update(weight, moment, average, grad, rate):
    moment_new = momentum_rate * moment + grad
    weight_new = weight - rate * (grad + momentum_rate * moment_new)
    average_new = average_rate * average + (1.0 - average_rate) * weight_new
    return (weight_new, moment_new, average_new)


def merge_stats(first, second):
    top = jnp.maximum(first[0], second[0])
    total = first[1] * jnp.exp(first[0] - top) + second[1] * jnp.exp(second[0] - top)
    return (top, total, first[2] + second[2])


def keep_same(args):
    return args


def contract_first(left, right):
    return lax.dot_general(
        left, right, (((1,), (1,)), ((), ())), preferred_element_type=jnp.float32
    )


def masked_scores(q_part, keys, q_index, k_index, span):
    scores = jnp.einsum(
        "qhd,kd->hqk", q_part, keys, preferred_element_type=jnp.float32
    ) * keys.shape[-1] ** (-0.5)
    offset = jnp.arange(span, dtype=jnp.int32)
    allowed = (k_index * span + offset)[None, :] <= (q_index * span + offset)[:, None]
    return jnp.where(allowed[None], scores, -jnp.inf)


def local(
    token_ids,
    labels,
    answer_mask,
    pair_map,
    w_layer,
    w_vocab,
    gains,
    mom_layer,
    mom_vocab,
    mom_gains,
    avg_layer,
    avg_vocab,
    avg_gains,
):
    f32 = jnp.float32
    bf16 = jnp.bfloat16
    group, qg, ffg, vg = widths()
    attn_in = qg + 2 * HD
    layer_width = attn_in + qg + 3 * ffg
    n_ctx = lax.axis_size("ctx")
    n_head = lax.axis_size("head")
    place = lax.axis_index("ctx")
    shard = lax.axis_index("head")
    tok = token_ids.shape[0]
    nblk = 2 * SEQS
    span = tok // nblk
    length = n_ctx * tok // SEQS
    scale = HD ** (-0.5)
    first = pair_map[place]
    mirror = 2 * n_ctx - 1 - first
    local_rows = jnp.arange(tok, dtype=jnp.int32)
    positions = jnp.where(local_rows // span % 2 == 0, first, mirror) * span + local_rows % span
    cosine, sine = yarn_tables(positions.astype(f32), HD)
    vocab_send = w_vocab.astype(bf16)
    layer_full, vocab_full, gain_full = (
        lax.all_gather(w_layer.astype(bf16), "ctx", axis=0, tiled=True),
        lax.all_gather(vocab_send, "ctx", axis=0, tiled=True),
        lax.all_gather(gains.astype(bf16), "ctx", axis=0, tiled=True),
    )
    gain_f = gain_full.astype(f32)
    w_in = layer_full[:, :attn_in]
    w_out = layer_full[:, attn_in : attn_in + qg]
    w_gu = layer_full[:, attn_in + qg : attn_in + qg + 2 * ffg]
    w_down = layer_full[:, attn_in + qg + 2 * ffg :]
    w_head = vocab_full[:, :vg]
    offset_id = shard * vg
    local_ids = token_ids - offset_id
    inside = (local_ids >= 0) & (local_ids < vg)
    picked = jnp.take(vocab_full[:, vg:], jnp.where(inside, local_ids, 0), axis=1).T
    embedded = jnp.where(inside[:, None], picked, jnp.zeros_like(picked))
    x0 = lax.psum(embedded.astype(f32).astype(jnp.bfloat16), "head").astype(jnp.float32)
    a1 = norm(x0, gain_f[:, 0]).astype(bf16)
    raw = jnp.dot(a1, w_in, preferred_element_type=f32)

    def rotate(values):
        queries = rope(values[:, :qg].reshape(tok, group, HD), cosine[:, None, :], sine[:, None, :])
        keys = rope(values[:, qg : qg + HD], cosine, sine)
        return (queries, keys, values[:, qg + HD :])

    (q_f, k_f, v_f), rotate_back = jax.vjp(rotate, raw)
    q_blocks = q_f.astype(bf16).reshape(nblk, span, group, HD)
    kv_local = jnp.concatenate([k_f, v_f], axis=1).astype(bf16)
    kv_every, mask_every = (
        lax.all_gather(kv_local, "ctx", axis=0, tiled=True),
        lax.all_gather(answer_mask.astype(bf16), "ctx", axis=0, tiled=True),
    )
    count = jnp.sum(mask_every.astype(f32))
    kv_blocks = kv_every.reshape(n_ctx, nblk, span, 2 * HD)
    key_index = jnp.stack([pair_map, 2 * n_ctx - 1 - pair_map], axis=1)
    q_index = jnp.stack([first, mirror] * SEQS)

    def stat_step(carry, item):
        top, total = carry
        keys_dev, k_index = item
        for b in range(nblk):
            for half in range(2):
                kb = 2 * (b // 2) + half

                def stat_live(args):
                    top_b, total_b = args
                    s = masked_scores(
                        q_blocks[b], keys_dev[kb, :, :HD], q_index[b], k_index[half], span
                    )
                    new_top = jnp.maximum(top_b, jnp.max(s, axis=-1))
                    return (
                        new_top,
                        total_b * jnp.exp(top_b - new_top)
                        + jnp.sum(jnp.exp(s - new_top[..., None]), axis=-1),
                    )

                new = lax.cond(
                    k_index[half] <= q_index[b], stat_live, keep_same, (top[b], total[b])
                )
                top = top.at[b].set(new[0])
                total = total.at[b].set(new[1])
        return ((top, total), None)

    start_top = jnp.full((nblk, group, span), -jnp.inf, f32)
    start_total = jnp.zeros((nblk, group, span), f32)
    (top, total), _ = lax.scan(stat_step, (start_top, start_total), (kv_blocks, key_index))
    lse_attn = top + jnp.log(total)

    def out_step(acc, item):
        keys_dev, k_index = item
        for b in range(nblk):
            for half in range(2):
                kb = 2 * (b // 2) + half

                def out_live(acc_b):
                    s = masked_scores(
                        q_blocks[b], keys_dev[kb, :, :HD], q_index[b], k_index[half], span
                    )
                    probs = jnp.exp(s - lse_attn[b][..., None])
                    return acc_b + jnp.einsum(
                        "hqk,kd->hqd",
                        probs.astype(bf16),
                        keys_dev[kb, :, HD:],
                        preferred_element_type=f32,
                    )

                acc = acc.at[b].set(
                    lax.cond(k_index[half] <= q_index[b], out_live, keep_same, acc[b])
                )
        return (acc, None)

    acc, _ = lax.scan(out_step, jnp.zeros((nblk, group, span, HD), f32), (kv_blocks, key_index))
    attn_f = acc.transpose(0, 2, 1, 3).reshape(tok, qg)
    attn_b = attn_f.astype(bf16)
    y_attn = lax.psum(contract_first(attn_b, w_out).astype(jnp.bfloat16), "head").astype(
        jnp.float32
    )
    x1 = x0 + y_attn
    a2 = norm(x1, gain_f[:, 1]).astype(bf16)
    gate_up = jnp.dot(a2, w_gu, preferred_element_type=f32)

    def glu(values):
        return jax.nn.silu(values[:, :ffg]) * values[:, ffg:]

    hidden_f, glu_back = jax.vjp(glu, gate_up)
    hidden_b = hidden_f.astype(bf16)
    y_ffn = lax.psum(contract_first(hidden_b, w_down).astype(jnp.bfloat16), "head").astype(
        jnp.float32
    )
    x2 = x1 + y_ffn
    final_b = norm(x2, gain_f[:, 2]).astype(bf16)
    logits = jnp.dot(final_b, w_head, preferred_element_type=f32)
    row_top = jnp.max(logits, axis=-1)
    row_total = jnp.sum(jnp.exp(logits - row_top[:, None]), axis=-1)
    local_labels = labels - offset_id
    label_in = (local_labels >= 0) & (local_labels < vg)
    hit = (jnp.arange(vg, dtype=jnp.int32)[None, :] == local_labels[:, None]) & label_in[:, None]
    label_logit = jnp.sum(jnp.where(hit, logits, 0.0), axis=-1)
    top_all, total_all, label_all = merged((row_top, row_total, label_logit), "head", merge_stats)
    lse = top_all + jnp.log(total_all)
    valid = answer_mask.astype(f32)
    loss_part = jnp.sum(valid * (lse - label_all + z_weight * lse * lse)) / count
    soft = jnp.exp(logits - lse[:, None])
    dlog_b = (
        (valid / count)[:, None] * ((1.0 + 2.0 * z_weight * lse)[:, None] * soft - hit.astype(f32))
    ).astype(bf16)
    d_final = lax.psum(contract_first(dlog_b, w_head).astype(jnp.bfloat16), "head").astype(
        jnp.float32
    )
    _, final_back = jax.vjp(norm, x2, gain_f[:, 2])
    dx2, d_gain2 = final_back(d_final)
    dyf_b = dx2.astype(bf16)
    d_hidden = jnp.dot(dyf_b, w_down, preferred_element_type=f32)
    d_gate_up_b = glu_back(d_hidden)[0].astype(bf16)
    d_second = lax.psum(contract_first(d_gate_up_b, w_gu).astype(jnp.bfloat16), "head").astype(
        jnp.float32
    )
    _, second_back = jax.vjp(norm, x1, gain_f[:, 1])
    dx1_norm, d_gain1 = second_back(d_second)
    dx1 = dx2 + dx1_norm
    dya_b = dx1.astype(bf16)
    d_attn_b = jnp.dot(dya_b, w_out, preferred_element_type=f32).astype(bf16)
    d_blocks = d_attn_b.reshape(nblk, span, group, HD)
    delta = jnp.einsum(
        "bqhd,bqhd->bhq", d_blocks.astype(f32), attn_f.reshape(nblk, span, group, HD)
    )

    def back_step(dq, item):
        keys_dev, k_index = item
        dkv = jnp.zeros((nblk, span, 2 * HD), f32)
        for b in range(nblk):
            for half in range(2):
                kb = 2 * (b // 2) + half

                def back_live(args):
                    dq_b, dkv_b = args
                    keys = keys_dev[kb, :, :HD]
                    values = keys_dev[kb, :, HD:]
                    s = masked_scores(q_blocks[b], keys, q_index[b], k_index[half], span)
                    probs = jnp.exp(s - lse_attn[b][..., None])
                    grad_v = jnp.einsum(
                        "hqk,qhd->kd", probs.astype(bf16), d_blocks[b], preferred_element_type=f32
                    )
                    grad_p = jnp.einsum(
                        "qhd,kd->hqk", d_blocks[b], values, preferred_element_type=f32
                    )
                    grad_s = (probs * (grad_p - delta[b][..., None])).astype(bf16)
                    dq_new = dq_b + scale * jnp.einsum(
                        "hqk,kd->qhd", grad_s, keys, preferred_element_type=f32
                    )
                    grad_k = scale * jnp.einsum(
                        "hqk,qhd->kd", grad_s, q_blocks[b], preferred_element_type=f32
                    )
                    return (dq_new, dkv_b + jnp.concatenate([grad_k, grad_v], axis=-1))

                new = lax.cond(k_index[half] <= q_index[b], back_live, keep_same, (dq[b], dkv[kb]))
                dq = dq.at[b].set(new[0])
                dkv = dkv.at[kb].set(new[1])
        return (dq, dkv)

    dq, dkv_every = lax.scan(
        back_step, jnp.zeros((nblk, span, group, HD), f32), (kv_blocks, key_index)
    )
    dkv_own = lax.psum_scatter(
        dkv_every.reshape(n_ctx * tok, 2 * HD).astype(jnp.bfloat16),
        "ctx",
        scatter_dimension=0,
        tiled=True,
    ).astype(jnp.float32)
    d_raw_b = rotate_back((dq.reshape(tok, group, HD), dkv_own[:, :HD], dkv_own[:, HD:]))[0].astype(
        bf16
    )
    d_first = lax.psum(contract_first(d_raw_b, w_in).astype(jnp.bfloat16), "head").astype(
        jnp.float32
    )
    _, first_back = jax.vjp(norm, x0, gain_f[:, 0])
    dx0_norm, d_gain0 = first_back(d_first)
    dx0 = dx1 + dx0_norm
    embed_slot = jnp.where(inside, local_ids, vg)

    def outer(left, right):
        return lax.dot_general(
            left, right, (((0,), (0,)), ((), ())), preferred_element_type=jnp.float32
        )

    gain_term = jnp.stack([d_gain0, d_gain1, d_gain2], axis=1)
    parts = [
        outer(a1, d_raw_b),
        outer(dya_b, attn_b),
        outer(a2, d_gate_up_b),
        outer(dyf_b, hidden_b),
        outer(final_b, dlog_b),
    ]
    parts.append(jax.ops.segment_sum(dx0, embed_slot, vg + 1)[:vg].T)
    parts.append(gain_term)
    grads = lax.psum_scatter(
        jnp.concatenate(parts, axis=1).astype(jnp.bfloat16), "ctx", scatter_dimension=0, tiled=True
    ).astype(jnp.float32)
    grad_layer = grads[:, :layer_width]
    grad_vocab = grads[:, layer_width : layer_width + 2 * vg]
    grad_gain = grads[:, layer_width + 2 * vg :]
    squares = (
        jnp.sum(grad_layer * grad_layer)
        + jnp.sum(grad_vocab * grad_vocab)
        + jnp.sum(grad_gain * grad_gain) / n_head
    )
    total_sq, loss = lax.psum((squares, loss_part / n_head), ("ctx", "head"))
    grad_norm = jnp.sqrt(total_sq)
    factor = jnp.minimum(1.0, clip_level / grad_norm)
    base = 1.5 * math.sqrt(total_params()) / clip_level
    layer_new, layer_moment, layer_average = update(
        w_layer, mom_layer, avg_layer, factor * grad_layer, base * layer_spread(length)
    )
    vocab_new, vocab_moment, vocab_average = update(
        w_vocab, mom_vocab, avg_vocab, factor * grad_vocab, base * vocab_spread()
    )
    gains_new, gains_moment, gains_average = update(
        gains, mom_gains, avg_gains, factor * grad_gain, base * 0.1
    )
    return (
        layer_new,
        layer_moment,
        layer_average,
        layer_new.astype(bf16),
        vocab_new,
        vocab_moment,
        vocab_average,
        vocab_new.astype(bf16),
        gains_new,
        gains_moment,
        gains_average,
        gains_new.astype(bf16),
        loss,
        grad_norm,
    )


def solution(mesh):
    in_specs = (
        P("ctx"),
        P("ctx"),
        P("ctx"),
        P(),
        P("ctx", "head"),
        P("ctx", "head"),
        P("ctx", None),
        P("ctx", "head"),
        P("ctx", "head"),
        P("ctx", None),
        P("ctx", "head"),
        P("ctx", "head"),
        P("ctx", None),
    )
    out_specs = (
        P("ctx", "head"),
        P("ctx", "head"),
        P("ctx", "head"),
        P("ctx", "head"),
        P("ctx", "head"),
        P("ctx", "head"),
        P("ctx", "head"),
        P("ctx", "head"),
        P("ctx", None),
        P("ctx", None),
        P("ctx", None),
        P("ctx", None),
        P(),
        P(),
    )
    return jax.shard_map(local, mesh=mesh, in_specs=in_specs, out_specs=out_specs, check_vma=False)
```

profile of v0, /device:TPU:0, one launch (start us, length us, event | category | flops | bytes accessed | tf_op | source)
XLA Modules:
  0.0 3086.4 jit_solution(16151892121469663935)
XLA Ops:
  7.2 16.9 copy.201
  24.1 8.7 convert_element_type.296
  33.5 311.4 %all-gather.10.cloned.1.call-done = bf16[2048,16000]{0,1:T(8,128)(2,1)} async-done(((bf16[256,16000]{0,1:T(8,128)(2,1)}), bf16[2048,16000]{0,1:T(8,128)(2,1)}) %all-gather.10.cloned.1.call-update) | async-done | bytes 65536016 | tf_op jit(solution)/shard_map/all_gather | solution.py:153
  344.9 22.7 slice.1746
  367.5 10.3 gather_fusion
  385.4 8.9 all_gather.34
  395.1 35.7 %all-reduce.18.cloned.1.call-done = bf16[256,2048]{1,0:T(8,128)(2,1)} async-done(((bf16[256,2048]{1,0:T(8,128)(2,1)}), bf16[256,2048]{1,0:T(8,128)(2,1)}) %all-reduce.18.cloned.1.call-update) | async-done | bytes 1048592 | tf_op jit(solution)/shard_map/psum | solution.py:167
  432.3 112.1 %all-gather.12.cloned.1.call-done = bf16[2048,5376]{1,0:T(8,128)(2,1)} async-done(((bf16[256,5376]{1,0:T(8,128)(2,1)}), bf16[2048,5376]{1,0:T(8,128)(2,1)}) %all-gather.12.cloned.1.call-update) | async-done | bytes 22020112 | tf_op jit(solution)/shard_map/all_gather | solution.py:152
  550.5 10.0 all_gather.36
  560.5 118.1 %while.97 = (s32[]{:T(128)}, f32[4,8,64]{2,1,0:T(8,128)S(1)}, f32[4,8,64]{2,1,0:T(8,128)S(1)}, s32[8,2]{1,0:T(8,128)S(1)}, s32[1]{0:T(128)}, /*index=5*/bf16[8,4...) while((s32[]{:T(128)}, f32[4,8,64]{2,1,0:T(8,128)S(1)}, ...), condition=%wide.region_35.36_spmd, body=%wide.region_2.35_spmd.sunk | while | flops 34907160 | bytes 3867729 | solution.py:216
  678.7 74.8 %while.98 = (s32[]{:T(128)}, f32[4,8,64,64]{3,2,1,0:T(8,128)S(1)}, s32[8,2]{1,0:T(8,128)S(1)}, s32[1]{0:T(128)}, bf16[8,4,64,128]{3,2,1,0:T(8,128)(2,1)S(1)}, /*...) while((s32[]{:T(128)}, f32[4,8,64,64]{3,2,1,0:T(8,128)S(1)}, ...), condition=%wide.region_54.55_spmd, body=%wide.region_37.54_spmd.sunk | while | flops 68453392 | bytes 10003377 | solution.py:242
  758.3 76.2 %all-reduce.20.cloned.1.call-done = bf16[256,2048]{1,0:T(8,128)(2,1)} async-done(((bf16[256,2048]{1,0:T(8,128)(2,1)}), bf16[256,2048]{1,0:T(8,128)(2,1)}) %all-reduce.20.cloned.1.call-update) | async-done | bytes 1048592 | tf_op jit(solution)/shard_map/psum | solution.py:245
  836.3 6.4 fusion.438
  850.5 9.2 all-gather.3
  860.3 41.4 %all-reduce.22.cloned.1.call-done = bf16[256,2048]{1,0:T(8,128)(2,1)} async-done(((bf16[256,2048]{1,0:T(8,128)(2,1)}), bf16[256,2048]{1,0:T(8,128)(2,1)}) %all-reduce.22.cloned.1.call-update) | async-done | bytes 1048592 | tf_op jit(solution)/shard_map/psum | solution.py:257
  903.5 18.5 fusion.534
  927.1 9.3 all-gather.5
  936.3 7.9 all-gather.6
  944.3 9.2 all-gather.4
  955.0 17.9 fusion.448
  973.5 6.1 copy.219
  979.6 16.9 copy.221
  996.5 17.0 copy.223
  1013.4 6.1 copy.218
  1035.0 8.4 fusion.445
  1043.7 18.0 convolution_convert_fusion
  1063.0 31.7 %all-reduce.26.cloned.1.call-done = bf16[256,2048]{1,0:T(8,128)(2,1)} async-done(((bf16[256,2048]{1,0:T(8,128)(2,1)}), bf16[256,2048]{1,0:T(8,128)(2,1)}) %all-reduce.26.cloned.1.call-update) | async-done | bytes 1048592 | tf_op jit(solution)/shard_map/psum | solution.py:285
  1107.3 348.0 %while.100 = (s32[]{:T(128)}, f32[4,64,8,64]{3,1,2,0:T(8,128)}, bf16[8,4,64,128]{3,2,1,0:T(8,128)(2,1)}, s32[8,2]{1,0:T(8,128)S(1)}, s32[1]{0:T(128)}, /*index=5...) while((s32[]{:T(128)}, f32[4,64,8,64]{3,1,2,0:T(8,128)}, ...), condition=%wide.region_85.86_spmd, body=%wide.region_68.85_spmd.sunk | while | flops 170320912 | bytes 24750540 | solution.py:331
  1457.4 8.3 convolution_convert_fusion.1
  1465.7 15.2 copy.217
  1484.3 12.8 reduce-scatter.4.cloned.1.call-done
  1511.8 43.1 %all-reduce.28.cloned.1.call-done = bf16[256,2048]{1,0:T(8,128)(2,1)} async-done(((bf16[256,2048]{1,0:T(8,128)(2,1)}), bf16[256,2048]{1,0:T(8,128)(2,1)}) %all-reduce.28.cloned.1.call-update) | async-done | bytes 1048592 | tf_op jit(solution)/shard_map/psum | solution.py:343
  1560.5 20.7 broadcast_in_dim.409
  1581.2 50.5 %scatter_fusion = f32[8001,2048]{1,0:T(8,128)} fusion(f32[8001,2048]{1,0:T(8,128)} %broadcast_in_dim.409, s32[256]{0:T(256)S(1)} %copy-done.51, f32[256,2048]{1,0:T(8,128)S(1)} %copy-done.16), kind=kCustom, calls=%fused_computation.1 | custom fusion | flops 524288 | bytes 6292480 | tf_op jit(solution)/shard_map/scatter-add | solution.py:364
  1631.7 31.9 %fusion.431 = bf16[2048,8000]{0,1:T(8,128)(2,1)} fusion(f32[8001,2048]{1,0:T(8,128)} %scatter_fusion), kind=kLoop, calls=%fused_computation.658 | loop fusion | bytes 65536000 | tf_op jit(solution)/shard_map/transpose | solution.py:364
  1663.6 352.5 %concatenate.149 = bf16[2048,21379]{0,1:T(8,128)(2,1)} concatenate(bf16[2048,640]{0,1:T(8,128)(2,1)S(1)} %copy-done.13, bf16[2048,512]{0,1:T(8,128)(2,1)} %convolution_convert_fusion.4, bf16[2048,2816]{0,1:T(8,128)(2,1)} %copy.217, bf16[2048,1408]{0,1:T(8,128)(2,1)} %convolution_convert_fusion.2, bf16[2048,8000]{0,1:T(8,128)(2,1)} %convolution_convert_fusion, ...), dimensions={1} | concatenate | bytes 175136768 | tf_op jit(solution)/shard_map/concatenate | solution.py:367
  2016.1 850.9 %reduce_scatter.22 = bf16[256,21379]{0,1:T(8,128)(2,1)} reduce-scatter(bf16[2048,21379]{0,1:T(8,128)(2,1)} %concatenate.149), channel_id=1, replica_groups=mesh['ctx'=8,'head'=4] {'ctx'}, use_global_device_ids=true, dimensions={0}, to_apply=%region_93.94 | reduce-scatter | bytes 98514432 | tf_op jit(solution)/shard_map/reduce_scatter | solution.py:366
  2867.1 6.1 convert_element_type.331
  2883.5 6.2 copy.220
  2889.6 38.1 %all-reduce.10 = (f32[]{:T(128)}, f32[]{:T(128)}) all-reduce(f32[]{:T(128)S(6)} %add.903, f32[]{:T(128)S(6)} %div.118), channel_id=1, replica_groups=mesh['ctx'=8,'head'=4] {'ctx','head'}, use_global_device_ids=true, to_apply=%region_97.98 | all-reduce | flops 2 | bytes 16 | tf_op jit(solution)/shard_map/psum | solution.py:377
  2929.8 29.8 fusion.519
  2959.6 16.9 copy.228
  2976.5 17.5 add_multiply_fusion
  2994.0 16.9 copy.230
  3010.8 16.9 copy.229
  3027.7 11.6 copy.231
  3039.3 9.9 fusion.520
  3055.3 7.3 add_multiply_fusion.1
  (1859 shorter events, 725.6 us)
Async XLA Ops:
  7.2 337.7 %all-gather.10.cloned.1.call-start = ((), (), s32[]{:S(2)}) async-start(), calls=%async_computation.2 | async-start | bytes 73728000 | tf_op jit(solution)/shard_map/all_gather | solution.py:153
  32.8 397.9 %all-reduce.18.cloned.1.call-start = ((), (), s32[]{:S(2)}) async-start(), calls=%async_computation.3 | async-start | bytes 2097152 | tf_op jit(solution)/shard_map/psum | solution.py:167
  379.0 165.4 %all-gather.12.cloned.1.call-start = ((), (), s32[]{:S(2)}) async-start(), calls=%async_computation.4 | async-start | bytes 24772608 | tf_op jit(solution)/shard_map/all_gather | solution.py:152
  383.4 451.1 %all-reduce.20.cloned.1.call-start = ((), (), s32[]{:S(2)}) async-start(), calls=%async_computation.5 | async-start | bytes 2097152 | tf_op jit(solution)/shard_map/psum | solution.py:245
  394.4 153.8 %copy-start.57 = (f32[32]{0:T(128)}, f32[32]{0:T(128)S(1)}, u32[]{:S(2)}) copy-start(f32[32]{0:T(128)S(1)} %multiply_add_fusion.14) | copy-start | bytes 388
  395.0 153.2 %copy-start.47 = (f32[256]{0:T(256)}, f32[256]{0:T(256)S(1)}, u32[]{:S(2)}) copy-start(f32[256]{0:T(256)S(1)} %fusion.509) | copy-start | bytes 3076
  395.0 149.4 %copy-start.36 = (f32[2048,1]{0,1:T(1,128)}, f32[2048,1]{0,1:T(1,128)S(1)}, u32[]{:S(2)}) copy-start(f32[2048,1]{0,1:T(1,128)S(1)} %get-tuple-element.2405) | copy-start | bytes 24580
  395.1 702.7 %copy-start.34 = (f32[2048,1]{0,1:T(1,128)}, f32[2048,1]{0,1:T(1,128)S(1)}, u32[]{:S(2)}) copy-start(f32[2048,1]{0,1:T(1,128)S(1)} %get-tuple-element.2403) | copy-start | bytes 24580
  432.3 112.2 %copy-start.49 = (f32[256]{0:T(256)}, f32[256]{0:T(256)S(1)}, u32[]{:S(2)}) copy-start(f32[256]{0:T(256)S(1)} %fusion.471) | copy-start | bytes 3076
  432.3 112.1 %copy-start.40 = (f32[256]{0:T(256)}, f32[256]{0:T(256)S(1)}, u32[]{:S(2)}) copy-start(f32[256]{0:T(256)S(1)} %fusion.513) | copy-start | bytes 3076
  754.8 79.7 %copy-start.1 = (bf16[256,2048]{1,0:T(8,128)(2,1)S(1)}, bf16[256,2048]{1,0:T(8,128)(2,1)}, u32[]{:S(2)}) copy-start(bf16[256,2048]{1,0:T(8,128)(2,1)} %all-reduce.18.cloned.1.call-done) | copy-start | bytes 3145732
  758.3 143.4 %all-reduce.22.cloned.1.call-start = ((), (), s32[]{:S(2)}) async-start(), calls=%async_computation.6 | async-start | bytes 2097152 | tf_op jit(solution)/shard_map/psum | solution.py:257
  836.3 261.5 %copy-start.39 = (f32[256]{0:T(256)}, f32[256]{0:T(256)S(1)}, u32[]{:S(2)}) copy-start(f32[256]{0:T(256)S(1)} %fusion.514) | copy-start | bytes 3076
  844.6 5.7 copy-start.24
  844.7 5.8 copy-start.60
  844.7 15.6 copy-start.59
  850.4 172.7 %all-reduce.24.cloned.1.call-start = ((), (), s32[]{:S(2)}) async-start(), calls=%async_computation.7 | async-start | bytes 2097152 | tf_op jit(solution)/shard_map/psum | solution.py:277
  972.9 121.8 %all-reduce.26.cloned.1.call-start = ((), (), s32[]{:S(2)}) async-start(), calls=%async_computation.8 | async-start | bytes 2097152 | tf_op jit(solution)/shard_map/psum | solution.py:285
  1043.5 453.6 %reduce-scatter.4.cloned.1.call-start = ((), (), s32[]{:S(2)}) async-start(), calls=%async_computation.9 | async-start | bytes 589824 | tf_op jit(solution)/shard_map/reduce_scatter | solution.py:334
  1107.3 8.1 copy-start.53
  1147.4 10.0 copy-start.54
  1157.4 8.2 copy-start.53
  1193.6 5.9 copy-start.54
  1233.1 10.0 copy-start.54
  1243.1 8.2 copy-start.53
  1279.3 5.9 copy-start.54
  1285.2 8.2 copy-start.53
  1321.5 5.9 copy-start.54
  1361.0 10.0 copy-start.54
  1371.0 8.2 copy-start.53
  1407.2 5.9 copy-start.54
  1413.1 8.2 copy-start.53
  1449.3 5.9 copy-start.54
  1457.3 97.6 %all-reduce.28.cloned.1.call-start = ((), (), s32[]{:S(2)}) async-start(), calls=%async_computation.10 | async-start | bytes 2097152 | tf_op jit(solution)/shard_map/psum | solution.py:343
  1465.7 15.3 copy-start.43
  1465.7 15.3 copy-start.5
  1482.3 15.6 copy-start.48
  1482.3 15.6 copy-start.58
  1511.7 45.6 %copy-start.50 = (f32[256]{0:T(256)S(1)}, f32[256]{0:T(256)}, u32[]{:S(2)}) copy-start(f32[256]{0:T(256)} %copy-done.49) | copy-start | bytes 3076
  1560.5 20.7 copy-start.16
  1560.5 20.7 copy-start.51
  1631.7 31.9 %copy-start.13 = (bf16[2048,640]{0,1:T(8,128)(2,1)S(1)}, bf16[2048,640]{0,1:T(8,128)(2,1)}, u32[]{:S(2)}) copy-start(bf16[2048,640]{0,1:T(8,128)(2,1)} %convolution_convert_fusion.3) | copy-start | bytes 7864324
  2873.2 7.7 copy-start
  2883.4 45.0 %copy-start.46 = (f32[256,3]{0,1:T(4,128)S(1)}, f32[256,3]{0,1:T(4,128)}, u32[]{:S(2)}) copy-start(f32[256,3]{0,1:T(4,128)} %param.155) | copy-start | bytes 9220
  2883.4 45.0 %copy-start.56 = (f32[256,3]{0,1:T(4,128)S(1)}, f32[256,3]{0,1:T(4,128)}, u32[]{:S(2)}) copy-start(f32[256,3]{0,1:T(4,128)} %param.158) | copy-start | bytes 9220
  2883.5 46.3 %copy-start.35 = (f32[16000]{0:T(1024)S(1)}, f32[16000]{0:T(1024)}, u32[]{:S(2)}) copy-start(f32[16000]{0:T(1024)} %select_multiply_fusion) | copy-start | bytes 192004
  2929.8 147.9 %copy-start.44 = (f32[256,3]{0,1:T(4,128)}, f32[256,3]{0,1:T(4,128)S(1)}, u32[]{:S(2)}) copy-start(f32[256,3]{0,1:T(4,128)S(1)} %get-tuple-element.2287) | copy-start | bytes 9220
  3027.7 11.6 copy-start.38
  (51 other events, 113.5 us)
Sparse Core Ops, SparseCore 0:
  32.9 311.8 all-gather.9
  379.1 51.5 all-reduce.17
  433.2 111.1 all-gather.11
  758.4 76.0 all-reduce.19
  850.5 51.1 all-reduce.21
  973.1 50.0 all-reduce.23
  1043.6 51.1 all-reduce.25
  1457.5 39.5 reduce-scatter.3
  1503.0 51.8 all-reduce.27
where the time goes:
time: 3120 us; the launch traced here: 3090 us
  blocking collectives  944 us (30%)
  local copies, waits for them, and re-layouts  923 us (30%)
  waiting for transfers between devices  666 us (21%)
  other arithmetic  203 us (7%)
  matrix products  175 us (6%)
  loops' own time  153 us (5%)
    reduce_scatter x1, blocking collectives, local(): lax.psum_scatter(jnp.concatenate(parts, axis=1).astype(jnp.bfloat16), 'ct...  851 us
    concatenate x1, local copies, waits for them, and re-layouts, local(): jnp.concatenate(parts, axis=1).astype(jnp.bfloat16)  353 us
    all_gather x1, waiting for transfers between devices, local(): lax.all_gather(vocab_send, 'ctx', axis=0, tiled=True)  311 us
    unnamed x136, local copies, waits for them, and re-layouts  161 us
    all_gather x1, waiting for transfers between devices, local(): lax.all_gather(w_layer.astype(bf16), 'ctx', axis=0, tiled=True)  112 us
    psum x1, waiting for transfers between devices, local(): lax.psum(contract_first(attn_b, w_out).astype(jnp.bfloat16), 'head')  76.2 us
    scatter x64, local copies, waits for them, and re-layouts, back_step(): dq = dq.at[b].set(new[0])  68.9 us
  transfers between devices with their start and end apart: 9, of which 9 were waited for; matrix products, arithmetic and copies ran while one was open for 4% of the time, Pallas kernels for 0%

commit v1 on v0

--- a/solution.py
+++ b/solution.py
@@ -16,6 +16,19 @@
 momentum_rate = 0.5
 average_rate = 0.5
 clip_level = 0.01
+
+
+def collect(x, axis, dim):
+    ways = lax.axis_size(axis)
+    up = [(d, (d + 1) % ways) for d in range(ways)]
+    down = [(d, (d - 1) % ways) for d in range(ways)]
+    earlier, later = ([x], [x])
+    for _ in range(ways // 2):
+        earlier.append(lax.ppermute(earlier[-1], axis, up))
+    for _ in range((ways - 1) // 2):
+        later.append(lax.ppermute(later[-1], axis, down))
+    line = jnp.concatenate([*earlier[::-1], *later[1:]], axis=dim)
+    return jnp.roll(line, (lax.axis_index(axis) - ways // 2) * x.shape[dim], axis=dim)
 
 
 def merged(value, axis, join):
@@ -150,7 +163,7 @@
     vocab_send = w_vocab.astype(bf16)
     layer_full, vocab_full, gain_full = (
         lax.all_gather(w_layer.astype(bf16), "ctx", axis=0, tiled=True),
-        lax.all_gather(vocab_send, "ctx", axis=0, tiled=True),
+        collect(vocab_send, "ctx", 0),
         lax.all_gather(gains.astype(bf16), "ctx", axis=0, tiled=True),
     )
     gain_f = gain_full.astype(f32)

time: 3120 us -> 3550 us (1.14)
  waiting for transfers between devices: 666 us -> 923 us
  local copies, waits for them, and re-layouts: 923 us -> 1070 us
    ppermute x0 -> x7, waiting for transfers between devices: none -> 620 us  [the longest x4 620 us: collect(): earlier.append(lax.ppermute(earlier[-1], axis, up))]
    all_gather x1 -> x0, waiting for transfers between devices: 311 us -> none  [local(): lax.all_gather(vocab_send, 'ctx', axis=0, tiled=True)]
    unnamed x136 -> x157, local copies, waits for them, and re-layouts: 161 us -> 251 us
    all_gather x1, waiting for transfers between devices: 112 us -> 62.4 us  [local(): lax.all_gather(w_layer.astype(bf16), 'ctx', axis=0, tiled=True)]
  transfers between devices with their start and end apart: 9 -> 15, of which waited for: 9 -> 12; matrix products, arithmetic and copies ran while one was open for 4% -> 4% of each run, Pallas kernels for 0% -> 0%
where the time goes in v1:
time: 3550 us; the launch traced here: 3510 us
  local copies, waits for them, and re-layouts  1070 us (30%)
  blocking collectives  943 us (27%)
  waiting for transfers between devices  923 us (26%)
  other arithmetic  215 us (6%)
  matrix products  177 us (5%)
  loops' own time  155 us (4%)
    reduce_scatter x1, blocking collectives, local(): lax.psum_scatter(jnp.concatenate(parts, axis=1).astype(jnp.bfloat16), 'ct...  851 us
    ppermute x4, waiting for transfers between devices, collect(): earlier.append(lax.ppermute(earlier[-1], axis, up))  620 us
    concatenate x1, local copies, waits for them, and re-layouts, local(): jnp.concatenate(parts, axis=1).astype(jnp.bfloat16)  353 us
    unnamed x157, local copies, waits for them, and re-layouts  251 us
    psum x1, waiting for transfers between devices, local(): lax.psum(contract_first(attn_b, w_out).astype(jnp.bfloat16), 'head')  75.6 us
  transfers between devices with their start and end apart: 15, of which 12 were waited for; matrix products, arithmetic and copies ran while one was open for 4% of the time, Pallas kernels for 0%

profile of v1, /device:TPU:0, one launch (start us, length us, event | category | flops | bytes accessed | tf_op | source)
XLA Modules:
  0.0 3514.0 jit_solution(10518342720331383386)
XLA Ops:
  8.1 16.9 copy.201
  31.7 91.9 %collective-permute-done = bf16[256,16000]{0,1:T(8,128)(2,1)S(1)} collective-permute-done((bf16[256,16000]{0,1:T(8,128)(2,1)S(1)}, bf16[256,16000]{0,1:T(8,128)(2,1)S(1)}, u32[]{:S(2)}, u32[]{:S(2)}) %collective-permute-start) | collective-permute-done | bytes 8192032 | tf_op jit(solution)/shard_map/ppermute | solution.py:27
  129.6 175.1 %collective-permute-done.1 = bf16[256,16000]{0,1:T(8,128)(2,1)S(1)} collective-permute-done((bf16[256,16000]{0,1:T(8,128)(2,1)S(1)}, bf16[256,16000]{0,1:T(8,128)(2,1)S(1)}, u32[]{:S(2)}, u32[]{:S(2)}) %collective-permute-start.1) | collective-permute-done | bytes 8192032 | tf_op jit(solution)/shard_map/ppermute | solution.py:27
  310.7 176.8 %collective-permute-done.2 = bf16[256,16000]{0,1:T(8,128)(2,1)} collective-permute-done((bf16[256,16000]{0,1:T(8,128)(2,1)S(1)}, bf16[256,16000]{0,1:T(8,128)(2,1)}, u32[]{:S(2)}, u32[]{:S(2)}) %collective-permute-start.2) | collective-permute-done | bytes 8192032 | tf_op jit(solution)/shard_map/ppermute | solution.py:27
  490.2 176.5 %collective-permute-done.3 = bf16[256,16000]{0,1:T(8,128)(2,1)} collective-permute-done((bf16[256,16000]{0,1:T(8,128)(2,1)}, bf16[256,16000]{0,1:T(8,128)(2,1)}, u32[]{:S(2)}, u32[]{:S(2)}) %collective-permute-start.3) | collective-permute-done | bytes 8192032 | tf_op jit(solution)/shard_map/ppermute | solution.py:27
  666.7 7.2 constant_dynamic-update-slice_fusion.50
  674.0 8.0 constant_dynamic-update-slice_fusion.49
  758.5 7.1 constant_dynamic-update-slice_fusion.35
  765.6 22.7 dynamic-slice.358
  788.3 10.3 gather_fusion
  806.4 7.4 all_gather.30
  814.6 34.7 all-reduce.18.cloned.1.call-done
  851.1 62.4 %all-gather.9.cloned.1.call-done = bf16[2048,5376]{1,0:T(8,128)(2,1)} async-done(((bf16[256,5376]{1,0:T(8,128)(2,1)}), bf16[2048,5376]{1,0:T(8,128)(2,1)}) %all-gather.9.cloned.1.call-update) | async-done | bytes 22020112 | tf_op jit(solution)/shard_map/all_gather | solution.py:165
  919.4 11.3 all_gather.32
  930.7 136.4 %while.97 = (s32[]{:T(128)}, f32[4,8,64]{2,1,0:T(8,128)S(1)}, f32[4,8,64]{2,1,0:T(8,128)S(1)}, s32[8,2]{1,0:T(8,128)}, s32[1]{0:T(128)}, /*index=5*/bf16[8,4,64,...) while((s32[]{:T(128)}, f32[4,8,64]{2,1,0:T(8,128)S(1)}, ...), condition=%wide.region_35.36_spmd, body=%wide.region_2.35_spmd.sunk | while | flops 34907160 | bytes 3867729 | solution.py:229
  1067.2 93.0 %while.98 = (s32[]{:T(128)}, f32[4,8,64,64]{3,2,1,0:T(8,128)S(1)}, s32[8,2]{1,0:T(8,128)}, s32[1]{0:T(128)}, bf16[8,4,64,128]{3,2,1,0:T(8,128)(2,1)}, /*index=5*...) while((s32[]{:T(128)}, f32[4,8,64,64]{3,2,1,0:T(8,128)S(1)}, ...), condition=%wide.region_54.55_spmd, body=%wide.region_37.54_spmd.sunk | while | flops 68453392 | bytes 10003377 | solution.py:255
  1166.4 75.6 %all-reduce.20.cloned.1.call-done = bf16[256,2048]{1,0:T(8,128)(2,1)} async-done(((bf16[256,2048]{1,0:T(8,128)(2,1)}), bf16[256,2048]{1,0:T(8,128)(2,1)}) %all-reduce.20.cloned.1.call-update) | async-done | bytes 1048592 | tf_op jit(solution)/shard_map/psum | solution.py:258
  1258.5 9.1 all-gather.3
  1268.2 41.5 %all-reduce.22.cloned.1.call-done = bf16[256,2048]{1,0:T(8,128)(2,1)} async-done(((bf16[256,2048]{1,0:T(8,128)(2,1)}), bf16[256,2048]{1,0:T(8,128)(2,1)}) %all-reduce.22.cloned.1.call-update) | async-done | bytes 1048592 | tf_op jit(solution)/shard_map/psum | solution.py:270
  1311.5 18.5 fusion.536
  1335.1 9.3 all-gather.5
  1344.4 7.9 all-gather.6
  1352.3 9.3 all-gather.4
  1363.1 18.7 fusion.448
  1388.2 16.9 copy.221
  1405.1 16.9 copy.223
  1444.6 8.5 fusion.445
  1453.6 18.0 convolution_convert_fusion
  1472.9 31.5 all-reduce.26.cloned.1.call-done
  1519.7 360.6 %while.100 = (s32[]{:T(128)}, f32[4,64,8,64]{3,1,2,0:T(8,128)}, bf16[8,4,64,128]{3,2,1,0:T(8,128)(2,1)}, s32[8,2]{1,0:T(8,128)}, s32[1]{0:T(128)}, /*index=5*/bf...) while((s32[]{:T(128)}, f32[4,64,8,64]{3,1,2,0:T(8,128)}, ...), condition=%wide.region_85.86_spmd, body=%wide.region_68.85_spmd.sunk | while | flops 170320912 | bytes 24749972 | solution.py:344
  1882.5 8.3 convolution_convert_fusion.1
  1890.7 15.2 copy.217
  1909.8 11.6 reduce-scatter.4.cloned.1.call-done
  1936.2 43.1 %all-reduce.28.cloned.1.call-done = bf16[256,2048]{1,0:T(8,128)(2,1)} async-done(((bf16[256,2048]{1,0:T(8,128)(2,1)}), bf16[256,2048]{1,0:T(8,128)(2,1)}) %all-reduce.28.cloned.1.call-update) | async-done | bytes 1048592 | tf_op jit(solution)/shard_map/psum | solution.py:356
  1985.3 20.7 broadcast_in_dim.409
  2006.1 49.8 %scatter_fusion = f32[8001,2048]{1,0:T(8,128)} fusion(f32[8001,2048]{1,0:T(8,128)} %broadcast_in_dim.409, s32[256]{0:T(256)S(1)} %copy-done.46, f32[256,2048]{1,0:T(8,128)S(1)} %copy-done.12), kind=kCustom, calls=%fused_computation.1 | custom fusion | flops 524288 | bytes 6292480 | tf_op jit(solution)/shard_map/scatter-add | solution.py:377
  2055.8 31.9 fusion.431
  2087.7 353.4 %concatenate.156 = bf16[2048,21379]{0,1:T(8,128)(2,1)} concatenate(bf16[2048,640]{0,1:T(8,128)(2,1)} %convolution_convert_fusion.3, bf16[2048,512]{0,1:T(8,128)(2,1)S(1)} %copy-done.11, bf16[2048,2816]{0,1:T(8,128)(2,1)} %copy.217, bf16[2048,1408]{0,1:T(8,128)(2,1)} %convolution_convert_fusion.2, bf16[2048,8000]{0,1:T(8,128)(2,1)} %convolution_convert_fusion, ...), dimensions={1} | concatenate | bytes 175136768 | tf_op jit(solution)/shard_map/concatenate | solution.py:380
  2441.1 850.8 %reduce_scatter.22 = bf16[256,21379]{0,1:T(8,128)(2,1)} reduce-scatter(bf16[2048,21379]{0,1:T(8,128)(2,1)} %concatenate.156), channel_id=1, replica_groups=mesh['ctx'=8,'head'=4] {'ctx'}, use_global_device_ids=true, dimensions={0}, to_apply=%region_93.94 | reduce-scatter | bytes 98514432 | tf_op jit(solution)/shard_map/reduce_scatter | solution.py:379
  3314.5 38.3 %all-reduce.10 = (f32[]{:T(128)}, f32[]{:T(128)}) all-reduce(f32[]{:T(128)S(6)} %add.916, f32[]{:T(128)S(6)} %div.118), channel_id=1, replica_groups=mesh['ctx'=8,'head'=4] {'ctx','head'}, use_global_device_ids=true, to_apply=%region_97.98 | all-reduce | flops 2 | bytes 16 | tf_op jit(solution)/shard_map/psum | solution.py:390
  3354.9 29.8 fusion.521
  3384.7 16.9 copy.228
  3401.6 17.5 add_multiply_fusion
  3419.1 16.9 copy.230
  3436.0 16.9 copy.229
  3452.8 11.6 copy.231
  3464.5 10.1 fusion.522
  3480.6 7.3 add_multiply_fusion.1
  (1865 shorter events, 912.2 us)
Async XLA Ops:
  8.0 841.2 %all-reduce.18.cloned.1.call-start = ((), (), s32[]{:S(2)}) async-start(), calls=%async_computation.2 | async-start | bytes 2097152 | tf_op jit(solution)/shard_map/psum | solution.py:180
  24.9 462.6 %copy-start.48 = (s32[256]{0:T(256)S(1)}, s32[256]{0:T(256)}, u32[]{:S(2)}) copy-start(s32[256]{0:T(256)} %param.149) | copy-start | bytes 3076
  31.2 92.4 %collective-permute-start = (bf16[256,16000]{0,1:T(8,128)(2,1)S(1)}, bf16[256,16000]{0,1:T(8,128)(2,1)S(1)}, u32[]{:S(2)}, u32[]{:S(2)}) collective-permute-start(bf16[256,16000]{0,1:T(8,128)(2,1)S(1)} %convert_element_type.296), channel_id=1, source_target_pairs={{0,4},{4,8},{8,12},{12,16},{16,20},{20,24},{24,28},{28,0},{1,5},{5... | collective-permute-start | bytes 24576008 | tf_op jit(solution)/shard_map/ppermute | solution.py:27
  127.0 177.7 %collective-permute-start.1 = (bf16[256,16000]{0,1:T(8,128)(2,1)S(1)}, bf16[256,16000]{0,1:T(8,128)(2,1)S(1)}, u32[]{:S(2)}, u32[]{:S(2)}) collective-permute-start(bf16[256,16000]{0,1:T(8,128)(2,1)S(1)} %collective-permute-done), channel_id=1, source_target_pairs={{0,4},{4,8},{8,12},{12,16},{16,20},{20,24},{24,28},{28,0},{1,5},{5... | collective-permute-start | bytes 24576008 | tf_op jit(solution)/shard_map/ppermute | solution.py:27
  127.0 181.1 %collective-permute-start.4 = (bf16[256,16000]{0,1:T(8,128)(2,1)S(1)}, bf16[256,16000]{0,1:T(8,128)(2,1)}, u32[]{:S(2)}, u32[]{:S(2)}) collective-permute-start(bf16[256,16000]{0,1:T(8,128)(2,1)S(1)} %convert_element_type.296), channel_id=1, source_target_pairs={{0,28},{4,0},{8,4},{12,8},{16,12},{20,16},{24,20},{28,24},{1,29},{... | collective-permute-start | bytes 24576008 | tf_op jit(solution)/shard_map/ppermute | solution.py:29
  308.0 179.5 %collective-permute-start.2 = (bf16[256,16000]{0,1:T(8,128)(2,1)S(1)}, bf16[256,16000]{0,1:T(8,128)(2,1)}, u32[]{:S(2)}, u32[]{:S(2)}) collective-permute-start(bf16[256,16000]{0,1:T(8,128)(2,1)S(1)} %collective-permute-done.1), channel_id=1, source_target_pairs={{0,4},{4,8},{8,12},{12,16},{16,20},{20,24},{24,28},{28,0},{1,5},{5... | collective-permute-start | bytes 24576008 | tf_op jit(solution)/shard_map/ppermute | solution.py:27
  308.0 179.5 %collective-permute-start.5 = (bf16[256,16000]{0,1:T(8,128)(2,1)}, bf16[256,16000]{0,1:T(8,128)(2,1)}, u32[]{:S(2)}, u32[]{:S(2)}) collective-permute-start(bf16[256,16000]{0,1:T(8,128)(2,1)} %collective-permute-done.4), channel_id=1, source_target_pairs={{0,28},{4,0},{8,4},{12,8},{16,12},{20,16},{24,20},{28,24},{1,29},{... | collective-permute-start | bytes 24576008 | tf_op jit(solution)/shard_map/ppermute | solution.py:29
  487.5 179.2 %collective-permute-start.3 = (bf16[256,16000]{0,1:T(8,128)(2,1)}, bf16[256,16000]{0,1:T(8,128)(2,1)}, u32[]{:S(2)}, u32[]{:S(2)}) collective-permute-start(bf16[256,16000]{0,1:T(8,128)(2,1)} %collective-permute-done.2), channel_id=1, source_target_pairs={{0,4},{4,8},{8,12},{12,16},{16,20},{20,24},{24,28},{28,0},{1,5},{5... | collective-permute-start | bytes 24576008 | tf_op jit(solution)/shard_map/ppermute | solution.py:27
  487.5 224.9 %collective-permute-start.6 = (bf16[256,16000]{0,1:T(8,128)(2,1)}, bf16[256,16000]{0,1:T(8,128)(2,1)}, u32[]{:S(2)}, u32[]{:S(2)}) collective-permute-start(bf16[256,16000]{0,1:T(8,128)(2,1)} %collective-permute-done.5), channel_id=1, source_target_pairs={{0,28},{4,0},{8,4},{12,8},{16,12},{20,16},{24,20},{28,24},{1,29},{... | collective-permute-start | bytes 24576008 | tf_op jit(solution)/shard_map/ppermute | solution.py:29
  666.7 15.2 slice-start.6
  674.0 12.3 slice-start.4
  682.0 10.3 slice-start.1
  799.9 113.7 %all-gather.9.cloned.1.call-start = ((), (), s32[]{:S(2)}) async-start(), calls=%async_computation.3 | async-start | bytes 24772608 | tf_op jit(solution)/shard_map/all_gather | solution.py:165
  804.3 437.7 %all-reduce.20.cloned.1.call-start = ((), (), s32[]{:S(2)}) async-start(), calls=%async_computation.4 | async-start | bytes 2097152 | tf_op jit(solution)/shard_map/psum | solution.py:258
  813.8 103.8 %copy-start.51 = (f32[32]{0:T(128)}, f32[32]{0:T(128)S(1)}, u32[]{:S(2)}) copy-start(f32[32]{0:T(128)S(1)} %multiply_add_fusion.14) | copy-start | bytes 388
  814.5 103.1 %copy-start.42 = (f32[256]{0:T(256)}, f32[256]{0:T(256)S(1)}, u32[]{:S(2)}) copy-start(f32[256]{0:T(256)S(1)} %fusion.509) | copy-start | bytes 3076
  814.5 102.3 %copy-start.31 = (f32[2048,1]{0,1:T(1,128)}, f32[2048,1]{0,1:T(1,128)S(1)}, u32[]{:S(2)}) copy-start(f32[2048,1]{0,1:T(1,128)S(1)} %get-tuple-element.2405) | copy-start | bytes 24580
  814.5 692.7 %copy-start.29 = (f32[2048,1]{0,1:T(1,128)}, f32[2048,1]{0,1:T(1,128)S(1)}, u32[]{:S(2)}) copy-start(f32[2048,1]{0,1:T(1,128)S(1)} %get-tuple-element.2403) | copy-start | bytes 24580
  851.1 65.7 %copy-start.44 = (f32[256]{0:T(256)}, f32[256]{0:T(256)S(1)}, u32[]{:S(2)}) copy-start(f32[256]{0:T(256)S(1)} %fusion.471) | copy-start | bytes 3076
  851.1 65.7 %copy-start.35 = (f32[256]{0:T(256)}, f32[256]{0:T(256)S(1)}, u32[]{:S(2)}) copy-start(f32[256]{0:T(256)S(1)} %fusion.513) | copy-start | bytes 3076
  1160.3 90.2 %copy-start.3 = (f32[4,8,64,64]{3,2,1,0:T(8,128)}, f32[4,8,64,64]{3,2,1,0:T(8,128)S(1)}, u32[]{:S(2)}) copy-start(f32[4,8,64,64]{3,2,1,0:T(8,128)S(1)} %get-tuple-element.1947) | copy-start | bytes 1572868
  1160.3 81.7 %copy-start.1 = (bf16[256,2048]{1,0:T(8,128)(2,1)S(1)}, bf16[256,2048]{1,0:T(8,128)(2,1)}, u32[]{:S(2)}) copy-start(bf16[256,2048]{1,0:T(8,128)(2,1)} %all-reduce.18.cloned.1.call-done) | copy-start | bytes 3145732
  1162.9 87.5 %copy-start.23 = (bf16[256,512]{1,0:T(8,128)(2,1)}, bf16[256,512]{1,0:T(8,128)(2,1)S(1)}, u32[]{:S(2)}) copy-start(bf16[256,512]{1,0:T(8,128)(2,1)S(1)} %convert_element_type.307) | copy-start | bytes 786436
  1166.3 143.4 %all-reduce.22.cloned.1.call-start = ((), (), s32[]{:S(2)}) async-start(), calls=%async_computation.5 | async-start | bytes 2097152 | tf_op jit(solution)/shard_map/psum | solution.py:270
  1243.7 263.5 %copy-start.34 = (f32[256]{0:T(256)}, f32[256]{0:T(256)S(1)}, u32[]{:S(2)}) copy-start(f32[256]{0:T(256)S(1)} %fusion.514) | copy-start | bytes 3076
  1252.9 15.3 copy-start.53
  1252.9 56.9 %copy-start.2 = (bf16[256,2048]{1,0:T(8,128)(2,1)S(1)}, bf16[256,2048]{1,0:T(8,128)(2,1)}, u32[]{:S(2)}) copy-start(bf16[256,2048]{1,0:T(8,128)(2,1)} %all-reduce.20.cloned.1.call-done) | copy-start | bytes 3145732
  1258.5 173.6 %all-reduce.24.cloned.1.call-start = ((), (), s32[]{:S(2)}) async-start(), calls=%async_computation.6 | async-start | bytes 2097152 | tf_op jit(solution)/shard_map/psum | solution.py:290
  1381.8 122.6 %all-reduce.26.cloned.1.call-start = ((), (), s32[]{:S(2)}) async-start(), calls=%async_computation.7 | async-start | bytes 2097152 | tf_op jit(solution)/shard_map/psum | solution.py:298
  1453.1 468.3 %reduce-scatter.4.cloned.1.call-start = ((), (), s32[]{:S(2)}) async-start(), calls=%async_computation.8 | async-start | bytes 589824 | tf_op jit(solution)/shard_map/reduce_scatter | solution.py:347
  1882.4 96.9 %all-reduce.28.cloned.1.call-start = ((), (), s32[]{:S(2)}) async-start(), calls=%async_computation.9 | async-start | bytes 2097152 | tf_op jit(solution)/shard_map/psum | solution.py:356
  1890.7 15.2 copy-start.38
  1890.7 15.3 copy-start.4
  1890.7 17.1 copy-start.26
  1890.7 17.1 copy-start.28
  1906.0 16.3 copy-start.43
  1906.0 16.3 copy-start.52
  1906.4 20.9 copy-start.14
  1907.8 19.5 copy-start.19
  1931.6 50.0 %copy-start.45 = (f32[256]{0:T(256)S(1)}, f32[256]{0:T(256)}, u32[]{:S(2)}) copy-start(f32[256]{0:T(256)} %copy-done.44) | copy-start | bytes 3076
  1985.3 20.7 copy-start.12
  1985.3 20.7 copy-start.46
  2055.8 31.9 copy-start.11
  3308.3 45.2 %copy-start.41 = (f32[256,3]{0,1:T(4,128)S(1)}, f32[256,3]{0,1:T(4,128)}, u32[]{:S(2)}) copy-start(f32[256,3]{0,1:T(4,128)} %param.155) | copy-start | bytes 9220
  3308.3 45.2 %copy-start.50 = (f32[256,3]{0,1:T(4,128)S(1)}, f32[256,3]{0,1:T(4,128)}, u32[]{:S(2)}) copy-start(f32[256,3]{0,1:T(4,128)} %param.158) | copy-start | bytes 9220
  3308.4 46.5 %copy-start.30 = (f32[16000]{0:T(1024)S(1)}, f32[16000]{0:T(1024)}, u32[]{:S(2)}) copy-start(f32[16000]{0:T(1024)} %select_multiply_fusion) | copy-start | bytes 192004
  3354.9 149.8 %copy-start.39 = (f32[256,3]{0,1:T(4,128)}, f32[256,3]{0,1:T(4,128)S(1)}, u32[]{:S(2)}) copy-start(f32[256,3]{0,1:T(4,128)S(1)} %get-tuple-element.2287) | copy-start | bytes 9220
  3452.8 11.6 copy-start.33
  (45 other events, 151.3 us)
Sparse Core Ops, SparseCore 0:
  800.0 49.2 all-reduce.17
  1166.4 75.5 all-reduce.19
  1258.6 51.1 all-reduce.21
  1382.0 50.0 all-reduce.23
  1453.2 51.1 all-reduce.25
  1927.4 51.8 all-reduce.27
Sparse Core Ops, SparseCore 1:
  804.4 109.1 all-gather.8
  1882.5 38.9 reduce-scatter.3
